TPU v7x, 128 devices: a whole 4x4x4 slice. The times are simulated.
128 devices in a mesh: expert: 64 (over z, y, x_hi, core), dp: 2 (over x_lo).
Axes of the slice: x: 4 (x_hi: 2, x_lo: 2; x = x_hi * 2 + x_lo), y: 4, z: 4, core: 2. Of those that a mesh axis runs over, the one named last changes fastest.
Arguments:
- tokens: bfloat16 [8192, 4096], P(('expert', 'dp')), may hold values from -6 to 6
- expert_ids: int32 [8192, 8], P(('expert', 'dp')), may hold values from 0 to 127, all different within a row; in each aligned block of 64 rows (0 to 63, 64 to 127, ...) at most 8 rows name the same one
- gate_up: bfloat16 [128, 4096, 1536], P('expert', None, 'dp'), may hold values from -0.09375 to 0.09375
Outputs:
- factors: float32 [128, 768, 768], P('expert', 'dp')
Inputs may be any that keep to these rules, and one draw needn't show every extreme that they name: `expert_ids`: each token names 8 distinct experts. Within each device's aligned block of 64 tokens no expert is named more than 8 times, a bound that some block reaches.
All inputs are finite; a program needn't handle non-finite values.
Results may differ from a plain program's by a relative error of at most 0.004.
Values may be sent and summed in bfloat16 or wider, within the bound.
A program may use at most 192 MiB of HBM per device.

v0:
```python
import jax
import jax.numpy as jnp
from jax import lax
from jax.sharding import PartitionSpec as P

damping = 0.25


def project(rows, weight):
    return jnp.einsum("esd,edc->esc", rows, weight, preferred_element_type=jnp.float32)


def swiglu(both, width):
    return (jax.nn.silu(both[:, :, :width]) * both[:, :, width:]).astype(jnp.bfloat16)


def second_moment(hidden, scale, extra):
    gram = jnp.einsum("esf,esg->efg", hidden, hidden, preferred_element_type=jnp.float32)
    identity = jnp.eye(hidden.shape[2], dtype=jnp.float32)
    return gram * scale + extra * identity[None]


def upper_factor(moment):
    return jnp.swapaxes(jnp.linalg.cholesky(moment), 1, 2)


def on_device(tokens, expert_ids, gate_up):
    expert_axis = lax.axis_size("expert")
    replicas = lax.axis_size("dp")
    local_count = gate_up.shape[0]
    expert_count = local_count * expert_axis
    token_count, top_count = expert_ids.shape
    width_full = gate_up.shape[2] * replicas // 2
    width_part = width_full // replicas
    capacity = 2 * token_count * top_count // expert_count
    rows_mean = token_count * expert_axis * replicas * top_count // expert_count
    scale = 1.0 / rows_mean
    extra = damping * damping / replicas
    flat_ids = expert_ids.reshape(-1)
    onehot = (flat_ids[:, None] == jnp.arange(expert_count, dtype=jnp.int32)[None, :]).astype(
        jnp.int32
    )
    ranking = jnp.sum((jnp.cumsum(onehot, axis=0) - 1) * onehot, axis=1)
    target = flat_ids * capacity + ranking
    placing = jnp.arange(expert_count * capacity, dtype=jnp.int32)[:, None] == target[None, :]
    placing = jnp.any(
        placing.reshape(expert_count * capacity, token_count, top_count), axis=2
    ).astype(jnp.bfloat16)
    outgoing = jnp.dot(placing, tokens, preferred_element_type=jnp.float32).astype(jnp.bfloat16)
    outgoing = outgoing.reshape(expert_count, capacity, tokens.shape[1])
    arrived = lax.all_to_all(outgoing, "expert", split_axis=0, concat_axis=1, tiled=True)
    both = project(arrived, lax.all_gather(gate_up, "dp", axis=2, tiled=True))
    hidden = swiglu(both, width_full)
    local_moment = second_moment(hidden, scale, extra)
    total_moment = lax.psum(local_moment, "dp")
    factor = upper_factor(total_moment)
    position = lax.axis_index("dp")
    return lax.dynamic_slice_in_dim(factor, position * width_part, width_part, 1)


def solution(mesh):
    return jax.shard_map(
        on_device,
        mesh=mesh,
        in_specs=(P(("expert", "dp"), None), P(("expert", "dp"), None), P("expert", None, "dp")),
        out_specs=P("expert", "dp", None),
        check_vma=False,
    )
```

profile of v0, /device:TPU:1, one launch (start us, length us, event | category | flops | bytes accessed | tf_op | source)
XLA Modules:
  0.0 836.7 jit_solution(10531696009400579675)
XLA Ops:
  9.2 5.6 convert_bitcast_fusion
  14.8 12.7 %all-to-all-start = ((bf16[128,8,4096]{2,1,0:T(8,128)(2,1)}), bf16[128,8,4096]{2,1,0:T(8,128)(2,1)}, u32[]{:S(2)}, u32[]{:S(2)}) async-start(bf16[128,8,4096]{2,1,0:T(8,128)(2,1)} %convert_bitcast_fusion), calls=%async_computation | async-start | bytes 16777216 | tf_op jit(solution)/shard_map/all_to_all | solution.py:51
  28.2 176.0 %all-to-all-done = bf16[128,8,4096]{2,1,0:T(8,128)(2,1)} async-done(((bf16[128,8,4096]{2,1,0:T(8,128)(2,1)}), bf16[128,8,4096]{2,1,0:T(8,128)(2,1)}, u32[]{:S(2)}, u32[]{:S(2)}) %all-to-all-start) | async-done | bytes 8388640 | tf_op jit(solution)/shard_map/all_to_all | solution.py:51
  204.2 184.2 %all-gather.2.cloned.1.call-done = bf16[2,4096,1536]{2,1,0:T(8,128)(2,1)} async-done(((bf16[2,4096,768]{2,1,0:T(8,128)(2,1)}), bf16[2,4096,1536]{2,1,0:T(8,128)(2,1)}) %all-gather.2.cloned.1.call-update) | async-done | bytes 25165840 | tf_op jit(solution)/shard_map/all_gather | solution.py:52
  388.4 20.7 %fusion = f32[2,512,1536]{2,1,0:T(8,128)} fusion(bf16[2,4096,1536]{2,1,0:T(8,128)(2,1)} %all-gather.2.cloned.1.call-done, bf16[64,2,8,4096]{3,2,1,0:T(8,128)(2,1)} %bitcast.4), kind=kOutput, calls=%fused_computation | convolution fusion | flops 12884901888 | bytes 39845888 | tf_op jit(solution)/shard_map/esd,edc->esc/dot_general | solution.py:10
  409.1 9.1 %multiply_add_fusion = f32[2,768,768]{1,2,0:T(8,128)} fusion(f32[768,768]{0,1:T(8,128)S(1)} %fusion.7, f32[2,512,1536]{2,1,0:T(8,128)} %fusion), kind=kOutput, calls=%fused_computation.6 | convolution fusion | flops 1215037440 | bytes 13369344 | tf_op jit(solution)/shard_map/esf,esg->efg/dot_general | solution.py:18
  418.6 128.3 %all-reduce.3.cloned.1.call-done = f32[2,768,768]{1,2,0:T(8,128)} async-done(((f32[2,768,768]{1,2,0:T(8,128)}), f32[2,768,768]{1,2,0:T(8,128)}) %all-reduce.3.cloned.1.call-update) | async-done | bytes 4718608 | tf_op jit(solution)/shard_map/psum | solution.py:55
  546.9 6.2 copy.71
  553.1 4.4 fusion.3
  559.6 23.5 %custom-call.49 = f32[2,128,128]{2,1,0:T(8,128)S(1)} custom-call(f32[2,128,128]{2,1,0:T(8,128)S(1)} %cholesky.426), custom_call_target="Cholesky" | custom-call | tf_op jit(solution)/shard_map/jit(cholesky)/cholesky | solution.py:24
  583.1 19.8 %custom-call.50 = f32[2,1,128,128]{2,3,1,0:T(8,128)S(1)} custom-call(f32[2,1,128,128]{3,2,1,0:T(8,128)S(1)} %select_bitcast_fusion.4), custom_call_target="InvertDiagBlocksLowerTriangular" | custom-call | tf_op jit(solution)/shard_map/jit(cholesky)/cholesky | solution.py:24
  605.4 2.8 constant_dynamic-update-slice_fusion.5
  610.0 23.5 %custom-call.51 = f32[2,128,128]{2,1,0:T(8,128)S(1)} custom-call(f32[2,128,128]{2,1,0:T(8,128)S(1)} %cholesky.430), custom_call_target="Cholesky" | custom-call | tf_op jit(solution)/shard_map/jit(cholesky)/cholesky | solution.py:24
  634.2 19.7 %custom-call.52 = f32[2,1,128,128]{2,3,1,0:T(8,128)S(1)} custom-call(f32[2,1,128,128]{3,2,1,0:T(8,128)S(1)} %get-tuple-element.18), custom_call_target="InvertDiagBlocksLowerTriangular" | custom-call | tf_op jit(solution)/shard_map/jit(cholesky)/cholesky | solution.py:24
  655.3 2.5 convolution_subtract_fusion.1
  657.8 23.7 %custom-call.53 = f32[2,128,128]{2,1,0:T(8,128)S(1)} custom-call(f32[2,128,128]{2,1,0:T(8,128)S(1)} %cholesky.435), custom_call_target="Cholesky" | custom-call | tf_op jit(solution)/shard_map/jit(cholesky)/cholesky | solution.py:24
  682.2 19.7 %custom-call.54 = f32[2,1,128,128]{2,3,1,0:T(8,128)S(1)} custom-call(f32[2,1,128,128]{3,2,1,0:T(8,128)S(1)} %get-tuple-element.16), custom_call_target="InvertDiagBlocksLowerTriangular" | custom-call | tf_op jit(solution)/shard_map/jit(cholesky)/cholesky | solution.py:24
  703.2 2.7 convolution_subtract_fusion.2
  705.9 23.5 %custom-call.55 = f32[2,128,128]{2,1,0:T(8,128)S(1)} custom-call(f32[2,128,128]{2,1,0:T(8,128)S(1)} %cholesky.440), custom_call_target="Cholesky" | custom-call | tf_op jit(solution)/shard_map/jit(cholesky)/cholesky | solution.py:24
  730.1 20.1 %custom-call.56 = f32[2,1,128,128]{2,3,1,0:T(8,128)S(1)} custom-call(f32[2,1,128,128]{3,2,1,0:T(8,128)S(1)} %get-tuple-element.14), custom_call_target="InvertDiagBlocksLowerTriangular" | custom-call | tf_op jit(solution)/shard_map/jit(cholesky)/cholesky | solution.py:24
  751.2 2.5 convolution_subtract_fusion.3
  753.8 23.5 %custom-call.57 = f32[2,128,128]{2,1,0:T(8,128)S(1)} custom-call(f32[2,128,128]{2,1,0:T(8,128)S(1)} %cholesky.445), custom_call_target="Cholesky" | custom-call | tf_op jit(solution)/shard_map/jit(cholesky)/cholesky | solution.py:24
  777.9 19.7 %custom-call.58 = f32[2,1,128,128]{2,3,1,0:T(8,128)S(1)} custom-call(f32[2,1,128,128]{3,2,1,0:T(8,128)S(1)} %get-tuple-element.12), custom_call_target="InvertDiagBlocksLowerTriangular" | custom-call | tf_op jit(solution)/shard_map/jit(cholesky)/cholesky | solution.py:24
  800.7 23.6 %custom-call.59 = f32[2,128,128]{2,1,0:T(8,128)S(1)} custom-call(f32[2,128,128]{2,1,0:T(8,128)S(1)} %convolution_subtract_fusion.4), custom_call_target="Cholesky" | custom-call | tf_op jit(solution)/shard_map/jit(cholesky)/cholesky | solution.py:24
  (57 shorter events, 25.2 us)
Async XLA Ops:
  6.5 2.7 copy-start
  6.5 0.7 copy-start.3
  6.5 381.9 %all-gather.2.cloned.1.call-start = ((), (), s32[]{:S(2)}) async-start(), calls=%async_computation.1 | async-start | bytes 37748736 | tf_op jit(solution)/shard_map/all_gather | solution.py:52
  14.8 189.4 %all-to-all-start = ((bf16[128,8,4096]{2,1,0:T(8,128)(2,1)}), bf16[128,8,4096]{2,1,0:T(8,128)(2,1)}, u32[]{:S(2)}, u32[]{:S(2)}) async-start(bf16[128,8,4096]{2,1,0:T(8,128)(2,1)} %convert_bitcast_fusion), calls=%async_computation | async-start | bytes 16777216 | tf_op jit(solution)/shard_map/all_to_all | solution.py:51
  27.5 519.4 %all-reduce.3.cloned.1.call-start = ((), (), s32[]{:S(2)}) async-start(), calls=%async_computation.2 | async-start | bytes 9437184 | tf_op jit(solution)/shard_map/psum | solution.py:55
  557.4 2.1 copy-start.2
  825.6 4.1 copy-start.1
Sparse Core Ops, SparseCore 0:
  9.0 379.3 all-gather.1
  418.4 128.4 all-reduce.2
where the time goes:
time: 841 us; the launch traced here: 837 us
  waiting for transfers between devices  489 us (58%)
  other arithmetic  252 us (30%)
  matrix products  54.7 us (7%)
  between operations  13.8 us (2%)
  local copies, waits for them, and re-layouts  13.5 us (2%)
  starting transfers between devices  13.2 us (2%)
    another operation x23, other arithmetic, upper_factor(): return jnp.swapaxes(jnp.linalg.cholesky(moment), 1, 2)  244 us
    all_gather x1, waiting for transfers between devices, on_device(): both = project(arrived, lax.all_gather(gate_up, 'dp', axis=2, tiled=True))  184 us
    all_to_all x1, waiting for transfers between devices, on_device(): lax.all_to_all(outgoing, 'expert', split_axis=0, concat_axis=1, tiled=True)  176 us
    psum x1, waiting for transfers between devices, on_device(): total_moment = lax.psum(local_moment, 'dp')  128 us
    dot_general x1, matrix products, project(): jnp.einsum('esd,edc->esc', rows, weight, preferred_element_type=jnp.float32)  20.7 us
    another operation x10, matrix products, upper_factor(): return jnp.swapaxes(jnp.linalg.cholesky(moment), 1, 2)  19.3 us
  transfers between devices with their start and end apart: 3, of which 3 were waited for; matrix products, arithmetic and copies ran while one was open for 1% of the time, Pallas kernels for 0%

commit v1 on v0

v1 whole, which is shorter than its diff:
```python
import jax
import jax.numpy as jnp
from jax import lax
from jax.sharding import Mesh, PartitionSpec as P
from jax.experimental import pallas as pl
from jax.experimental.pallas import tpu as pltpu

damping = 0.25
capacity = 8
rows_mean = 512

N=768; B=128; NB=N//B
HI=lax.Precision.HIGHEST
def dotT(a,b):
    return lax.dot_general(a,b,(((0,),(0,)),((),())),precision=HI,preferred_element_type=jnp.float32)
def dot(a,b):
    return lax.dot_general(a,b,(((1,),(0,)),((),())),precision=HI,preferred_element_type=jnp.float32)
def factor_block(get, put_u, put_l):
    sub=lax.broadcasted_iota(jnp.int32,(8,128),0); lane=lax.broadcasted_iota(jnp.int32,(8,128),1)
    A=[get(i) for i in range(16)]
    E=[jnp.where(lane==sub+8*i,1.0,0.0).astype(jnp.float32) for i in range(16)]
    D=[jnp.zeros((8,128),jnp.float32) for i in range(16)]
    for j in range(128):
        q,s=divmod(j,8)
        cols=[jnp.broadcast_to(A[i][:,j:j+1],(8,128)) for i in range(q,16)]
        piv=jnp.broadcast_to(cols[0][s:s+1,:],(8,128))
        inv=1.0/piv
        D[q]=jnp.where(sub==s,piv,D[q])
        ra=jnp.broadcast_to(A[q][s:s+1,:],(8,128))*inv
        re=jnp.broadcast_to(E[q][s:s+1,:],(8,128))*inv
        for i in range(q,16):
            c=cols[i-q]
            if i==q:
                if s==7: continue
                c=jnp.where(sub>s,c,0.0)
            A[i]=A[i]-c*ra
            E[i]=E[i]-c*re
    for i in range(16):
        rs=lax.rsqrt(D[i])
        put_u(i, jnp.where(lane>=sub+8*i,A[i]*rs,0.0)); put_l(i, E[i]*rs)
def chol_kernel(g_ref, r_ref, a_ref, l_ref):
    a_ref[...]=g_ref[...]
    r_ref[...]=jnp.zeros_like(r_ref)
    for k in range(NB):
        o=k*B
        def put_u(i,v): r_ref[o+8*i:o+8*i+8,o:o+B]=v
        def put_l(i,v): l_ref[8*i:8*i+8,:]=v
        factor_block(lambda i:a_ref[o+8*i:o+8*i+8,o:o+B],put_u,put_l)
        if k<NB-1:
            p=dot(l_ref[...],a_ref[o:o+B,o+B:])
            r_ref[o:o+B,o+B:]=p
            for m in range(k+1,NB):
                x=m*B
                a_ref[x:x+B,x:]-=dotT(r_ref[o:o+B,x:x+B],r_ref[o:o+B,x:])
def upper_factor(g):
    return pl.pallas_call(chol_kernel,out_shape=jax.ShapeDtypeStruct((N,N),jnp.float32),
       in_specs=[pl.BlockSpec(memory_space=pltpu.VMEM)],out_specs=pl.BlockSpec(memory_space=pltpu.VMEM),
       scratch_shapes=[pltpu.VMEM((N,N),jnp.float32),pltpu.VMEM((B,B),jnp.float32)],
       compiler_params=pltpu.CompilerParams(vmem_limit_bytes=40<<20),name="upper_factor")(g)


def place(ids, names, capacity):
    blocks, tokens, _ = ids.shape
    named = jnp.any(ids[:, :, :, None] == names[None, None, None, :], axis=2)
    before = (jnp.arange(tokens)[:, None] > jnp.arange(tokens)[None, :]).astype(jnp.bfloat16)
    rank = jnp.einsum("st,btd->bsd", before, named.astype(jnp.bfloat16), preferred_element_type=jnp.float32)
    rank = jnp.where(named, rank.astype(jnp.int32), capacity)
    rank = rank.transpose(2, 0, 1)
    slot = jnp.arange(capacity, dtype=jnp.int32)
    block = jnp.arange(blocks, dtype=jnp.int32)
    chosen = (rank[:, None, None, :, :] == slot[None, None, :, None, None]) & (
        block[None, :, None, None, None] == block[None, None, None, :, None]
    )
    return chosen.astype(jnp.bfloat16).reshape(names.shape[0] * blocks * capacity, blocks * tokens)


def on_device(tokens, expert_ids, gate_up):
    z, y, c = lax.axis_index("z"), lax.axis_index("y"), lax.axis_index("core")
    xh, xl = lax.axis_index("xh"), lax.axis_index("xl")
    ring = ("xh", "xl")
    plane = ("z", "y", "core")
    width = gate_up.shape[2]
    send = lax.dynamic_index_in_dim(gate_up, 1 - xl, 0, keepdims=False)
    keep = lax.dynamic_index_in_dim(gate_up, xl, 0, keepdims=False)
    other = lax.ppermute(send, "xl", [(0, 1), (1, 0)])
    near = lax.all_gather(tokens, ring, axis=0, tiled=True)
    ids = lax.all_gather(expert_ids, ring, axis=0, tiled=True)
    ids = ids.reshape(4, tokens.shape[0], expert_ids.shape[1])
    d = jnp.arange(32, dtype=jnp.int32)
    names = (d // 2) * 8 + xh * 4 + (d % 2) * 2 + xl
    placing = place(ids, names, capacity)
    outgoing = jnp.dot(placing, near, preferred_element_type=jnp.float32).astype(jnp.bfloat16)
    rows = lax.all_to_all(outgoing.reshape(32, 32, tokens.shape[1]), plane, 0, 0, tiled=True)
    rows = rows.reshape(1024, tokens.shape[1])
    mine = jnp.dot(rows, keep, preferred_element_type=jnp.float32)
    theirs = jnp.dot(rows, other, preferred_element_type=jnp.float32)
    gate = jnp.where(xl == 0, mine, theirs)
    up = jnp.where(xl == 0, theirs, mine)
    hidden = (jax.nn.silu(gate) * up).astype(jnp.bfloat16)
    gram = lax.dot_general(hidden, hidden, (((0,), (0,)), ((), ())), preferred_element_type=jnp.float32)
    moment = gram * (1.0 / rows_mean) + damping * damping * jnp.eye(width, dtype=jnp.float32)
    factor = upper_factor(moment)
    half = width // 2
    away = lax.dynamic_slice_in_dim(factor, (1 - xl) * half, half, 0)
    here = lax.dynamic_slice_in_dim(factor, xl * half, half, 0)
    got = lax.ppermute(away, "xl", [(0, 1), (1, 0)])
    return jnp.stack([jnp.where(xl == 0, here, got), jnp.where(xl == 0, got, here)])


def solution(mesh):
    split = Mesh(mesh.devices.reshape(4, 4, 2, 2, 2), ("z", "y", "xh", "core", "xl"))
    every = ("z", "y", "xh", "core", "xl")
    experts = ("z", "y", "xh", "core")
    return jax.shard_map(
        on_device,
        mesh=split,
        in_specs=(P(every, None), P(every, None), P(experts, None, "xl")),
        out_specs=P(experts, "xl", None),
        check_vma=False,
    )
```

time: 841 us -> 378 us (0.45)
  waiting for transfers between devices: 489 us -> 176 us
  other arithmetic: 252 us -> 2.7 us
  Pallas kernels: 0 us -> 107 us
  blocking collectives: 0 us -> 10.4 us
  matrix products: 54.7 us -> 44.6 us
    another operation x25 -> x2, other arithmetic: 244 us -> 1.72 us  [on_device(): jnp.stack([jnp.where(xl == 0, here, got), jnp.where(xl == 0, got, here)])]
    all_gather x1, waiting for transfers between devices: 184 us -> 23.4 us  [on_device(): near = lax.all_gather(tokens, ring, axis=0, tiled=True)]
    psum x1 -> x0, waiting for transfers between devices: 128 us -> none  [on_device(): total_moment = lax.psum(local_moment, 'dp')]
    pallas_call x0 -> x1, Pallas kernels: none -> 107 us  [upper_factor(): pl.pallas_call(chol_kernel, out_shape=jax.ShapeDtypeStruct((N, N), jnp.fl...]
    all_to_all x1, waiting for transfers between devices: 176 us -> 93.6 us  [on_device(): lax.all_to_all(outgoing.reshape(32, 32, tokens.shape[1]), plane, 0, 0, ti...]
    ppermute x0 -> x2, waiting for transfers between devices: none -> 58.1 us  [the longest x1 31.8 us: on_device(): other = lax.ppermute(send, 'xl', [(0, 1), (1, 0)])]
    another operation x10 -> x0, matrix products: 19.3 us -> none  [upper_factor(): return jnp.swapaxes(jnp.linalg.cholesky(moment), 1, 2)]
    all_gather x0 -> x1, blocking collectives: none -> 10.4 us  [on_device(): ids = lax.all_gather(expert_ids, ring, axis=0, tiled=True)]
  transfers between devices with their start and end apart: 3 -> 4, of which waited for: 3 -> 4; matrix products, arithmetic and copies ran while one was open for 1% -> 5% of each run, Pallas kernels for 0% -> 0%
where the time goes in v1:
time: 378 us; the launch traced here: 372 us
  waiting for transfers between devices  176 us (47%)
  Pallas kernels  107 us (28%)
  matrix products  44.6 us (12%)
  between operations  13.7 us (4%)
  blocking collectives  10.4 us (3%)
  local copies, waits for them, and re-layouts  9.51 us (3%)
  starting transfers between devices  8.26 us (2%)
    pallas_call x1, Pallas kernels, upper_factor(): pl.pallas_call(chol_kernel, out_shape=jax.ShapeDtypeStruct((N, N), jnp.fl...  107 us
    all_to_all x1, waiting for transfers between devices, on_device(): lax.all_to_all(outgoing.reshape(32, 32, tokens.shape[1]), plane, 0, 0, ti...  93.6 us
    ppermute x1, waiting for transfers between devices, on_device(): other = lax.ppermute(send, 'xl', [(0, 1), (1, 0)])  31.8 us
    ppermute x1, waiting for transfers between devices, on_device(): got = lax.ppermute(away, 'xl', [(0, 1), (1, 0)])  26.3 us
    dot_general x1, matrix products, on_device(): lax.dot_general(hidden, hidden, (((0,), (0,)), ((), ())), preferred_eleme...  25.8 us
    all_gather x1, waiting for transfers between devices, on_device(): near = lax.all_gather(tokens, ring, axis=0, tiled=True)  23.4 us
    dot_general x1, matrix products, on_device(): mine = jnp.dot(rows, keep, preferred_element_type=jnp.float32)  11.4 us
    all_gather x1, blocking collectives, on_device(): ids = lax.all_gather(expert_ids, ring, axis=0, tiled=True)  10.4 us
  transfers between devices with their start and end apart: 4, of which 4 were waited for; matrix products, arithmetic and copies ran while one was open for 5% of the time, Pallas kernels for 0%

profile of v1, /device:TPU:1, one launch (start us, length us, event | category | flops | bytes accessed | tf_op | source)
XLA Modules:
  0.0 371.6 jit_solution(9314825691645136390)
XLA Ops:
  6.5 0.0 all-gather.3.cloned.1.call-start
  6.5 0.7 all-gather.3.cloned.1.call-update
  7.3 10.4 %all-gather = s32[4,64,8]{1,2,0:T(8,128)S(1)} all-gather(s32[1,64,8]{1,2,0:T(8,128)} %bitcast.28), channel_id=1, replica_groups=mesh['z'=4,'y'=4,'xh'=2,'core'=2,'xl'=2] {'xh','xl'}, dimensions={0}, use_global_device_ids=true | all-gather | bytes 10240 | tf_op jit(solution)/shard_map/all_gather | solution.py:87
  17.6 0.1 compare_reduce_fusion
  17.8 0.1 fusion.4
  18.0 0.1 iota_compare_fusion.1
  18.1 0.7 broadcast_and_fusion
  18.8 0.9 and.49
  19.7 23.4 %all-gather.3.cloned.1.call-done = bf16[256,4096]{1,0:T(8,128)(2,1)} async-done(((bf16[64,4096]{1,0:T(8,128)(2,1)}), bf16[256,4096]{1,0:T(8,128)(2,1)}) %all-gather.3.cloned.1.call-update) | async-done | bytes 2097168 | tf_op jit(solution)/shard_map/all_gather | solution.py:86
  43.1 7.2 %convolution_convert_fusion = bf16[1024,4096]{1,0:T(8,128)(2,1)} fusion(pred[1024,256]{1,0:T(32,128)(4,1)S(1)} %and.49, bf16[256,4096]{1,0:T(8,128)(2,1)} %all-gather.3.cloned.1.call-done), kind=kOutput, calls=%fused_computation | convolution fusion | flops 2151677952 | bytes 10747904 | tf_op jit(solution)/shard_map/dot_general | solution.py:92
  50.2 7.8 %all-to-all-start = ((bf16[32,32,4096]{2,1,0:T(8,128)(2,1)}), bf16[32,32,4096]{2,1,0:T(8,128)(2,1)}, u32[]{:S(2)}, u32[]{:S(2)}) async-start(bf16[32,32,4096]{2,1,0:T(8,128)(2,1)} %bitcast.27), calls=%async_computation | async-start | bytes 16777216 | tf_op jit(solution)/shard_map/all_to_all | solution.py:93
  58.0 5.8 %dynamic-slice_bitcast_fusion = bf16[4096,768]{1,0:T(8,128)(2,1)} fusion(bf16[2,4096,768]{2,1,0:T(8,128)(2,1)} %param.5, s32[]{:T(128)S(6)} %select_n.68), kind=kLoop, calls=%fused_computation.3 | loop fusion | bytes 12582916 | tf_op jit(solution)/shard_map/jit(dynamic_index_in_dim)/squeeze | solution.py:83
  63.8 0.3 collective-permute-start
  64.1 93.6 %all-to-all-done = bf16[32,32,4096]{2,1,0:T(8,128)(2,1)} async-done(((bf16[32,32,4096]{2,1,0:T(8,128)(2,1)}), bf16[32,32,4096]{2,1,0:T(8,128)(2,1)}, u32[]{:S(2)}, u32[]{:S(2)}) %all-to-all-start) | async-done | bytes 8388640 | tf_op jit(solution)/shard_map/all_to_all | solution.py:93
  157.7 11.4 %fusion = f32[1024,768]{1,0:T(8,128)S(1)} fusion(bf16[1024,4096]{1,0:T(8,128)(2,1)} %bitcast.5, bf16[2,4096,768]{2,1,0:T(8,128)(2,1)} %param.5, s32[]{:T(128)S(6)} %select_n.67), kind=kOutput, calls=%fused_computation.1 | convolution fusion | flops 6442450944 | bytes 17825796 | tf_op jit(solution)/shard_map/dot_general | solution.py:95
  169.2 31.8 %collective-permute-done = bf16[4096,768]{1,0:T(8,128)(2,1)} collective-permute-done((bf16[4096,768]{1,0:T(8,128)(2,1)}, bf16[4096,768]{1,0:T(8,128)(2,1)}, u32[]{:S(2)}, u32[]{:S(2)}) %collective-permute-start) | collective-permute-done | bytes 6291488 | tf_op jit(solution)/shard_map/ppermute | solution.py:85
  200.9 25.8 %select_add_fusion.g_ref = f32[768,768]{1,0:T(8,128)} fusion(f32[1024,768]{1,0:T(8,128)S(1)} %fusion, pred[]{:T(512)S(6)} %eq.62, bf16[1024,4096]{1,0:T(8,128)(2,1)} %bitcast.5, bf16[4096,768]{1,0:T(8,128)(2,1)} %collective-permute-done), kind=kOutput, calls=%fused_computation.7 | convolution fusion | flops 7659061248 | bytes 20185088 | tf_op jit(solution)/shard_map/dot_general | solution.py:100
  226.8 1.7 copy-done
  228.4 106.7 %upper_factor.1 = f32[768,768]{1,0:T(8,128)S(1)} custom-call(f32[768,768]{1,0:T(8,128)S(1)} %copy-done), custom_call_target="tpu_custom_call" | custom-call | tf_op jit(solution)/shard_map/upper_factor/pallas_call | solution.py:56
  335.1 1.1 constant_dynamic-slice_fusion
  336.2 0.2 collective-permute-start.1
  336.5 26.3 %collective-permute-done.1 = f32[384,768]{1,0:T(8,128)S(1)} collective-permute-done((f32[384,768]{1,0:T(8,128)}, f32[384,768]{1,0:T(8,128)S(1)}, u32[]{:S(2)}, u32[]{:S(2)}) %collective-permute-start.1) | collective-permute-done | bytes 1179680 | tf_op jit(solution)/shard_map/ppermute | solution.py:106
  362.7 0.2 select_bitcast_fusion.1
  362.9 1.6 pad_maximum_fusion
  (4 shorter events, 0.1 us)
Async XLA Ops:
  6.5 36.5 %all-gather.3.cloned.1.call-start = ((), (), s32[]{:S(2)}) async-start(), calls=%async_computation.1 | async-start | bytes 2621440 | tf_op jit(solution)/shard_map/all_gather | solution.py:86
  50.2 107.5 %all-to-all-start = ((bf16[32,32,4096]{2,1,0:T(8,128)(2,1)}), bf16[32,32,4096]{2,1,0:T(8,128)(2,1)}, u32[]{:S(2)}, u32[]{:S(2)}) async-start(bf16[32,32,4096]{2,1,0:T(8,128)(2,1)} %bitcast.27), calls=%async_computation | async-start | bytes 16777216 | tf_op jit(solution)/shard_map/all_to_all | solution.py:93
  63.8 137.1 %collective-permute-start = (bf16[4096,768]{1,0:T(8,128)(2,1)}, bf16[4096,768]{1,0:T(8,128)(2,1)}, u32[]{:S(2)}, u32[]{:S(2)}) collective-permute-start(bf16[4096,768]{1,0:T(8,128)(2,1)} %dynamic-slice_bitcast_fusion), channel_id=1, source_target_pairs={{0,1},{1,0},{2,3},{3,2},{4,5},{5,4},{6,7},{7,6},{8,9},{9,8},{10,11... | collective-permute-start | bytes 18874376 | tf_op jit(solution)/shard_map/ppermute | solution.py:85
  226.8 1.7 copy-start
  336.2 26.5 %collective-permute-start.1 = (f32[384,768]{1,0:T(8,128)}, f32[384,768]{1,0:T(8,128)S(1)}, u32[]{:S(2)}, u32[]{:S(2)}) collective-permute-start(f32[384,768]{1,0:T(8,128)} %constant_dynamic-slice_fusion), channel_id=1, source_target_pairs={{0,1},{1,0},{2,3},{3,2},{4,5},{5,4},{6,7},{7,6},{8,9},{9,8},{10,11... | collective-permute-start | bytes 3538952 | tf_op jit(solution)/shard_map/ppermute | solution.py:106
Sparse Core Ops, SparseCore 0:
  9.0 34.0 all-gather.2

commit v2 on v1

v2 whole, which is shorter than its diff:
```python
import jax
import jax.numpy as jnp
from jax import lax
from jax.sharding import Mesh, PartitionSpec as P
from jax.experimental import pallas as pl
from jax.experimental.pallas import tpu as pltpu

damping = 0.25
capacity = 8
rows_mean = 512
experts = 128
part = 128
in_kernel = 768
MESH = pl.DeviceIdType.MESH

N=768; B=128; NB=N//B
HI=lax.Precision.HIGHEST
def dotT(a,b):
    return lax.dot_general(a,b,(((0,),(0,)),((),())),precision=HI,preferred_element_type=jnp.float32)
def dot(a,b):
    return lax.dot_general(a,b,(((1,),(0,)),((),())),precision=HI,preferred_element_type=jnp.float32)
def rep(v,s):
    return jnp.broadcast_to(v[s:s+1,:],(8,128))
def factor_block(get, put_u, put_l):
    sub=lax.broadcasted_iota(jnp.int32,(8,128),0); lane=lax.broadcasted_iota(jnp.int32,(8,128),1)
    A=[get(i) for i in range(16)]
    E=[jnp.where(lane==sub+8*i,1.0,0.0).astype(jnp.float32) for i in range(16)]
    for q in range(16):
        C=[[jnp.broadcast_to(A[i][:,8*q+m:8*q+m+1],(8,128)) for m in range(8)] for i in range(q,16)]
        p={(j,m):rep(C[0][m],j) for j in range(8) for m in range(j,8)}
        t=[rep(A[q],j) for j in range(8)]
        e=[rep(E[q],j) for j in range(8)]
        pivot=jnp.zeros((8,128),jnp.float32)
        for j in range(8):
            inv=1.0/p[j,j]
            pivot=jnp.where(sub==j,p[j,j],pivot)
            f={m:p[j,m]*inv for m in range(j+1,8)}
            for k in range(j+1,8):
                for m in range(k,8):
                    p[k,m]=p[k,m]-p[j,k]*f[m]
            for m in range(j+1,8):
                t[m]=t[m]-f[m]*t[j]
                e[m]=e[m]-f[m]*e[j]
            ts=t[j]*inv; es=e[j]*inv
            for i in range(q+1,16):
                c=C[i-q]
                for m in range(j+1,8):
                    c[m]=c[m]-c[j]*f[m]
                A[i]=A[i]-c[j]*ts
                E[i]=E[i]-c[j]*es
        rs=lax.rsqrt(pivot)
        u=t[0]; l=e[0]
        for j in range(1,8):
            u=jnp.where(sub==j,t[j],u); l=jnp.where(sub==j,e[j],l)
        put_u(q, jnp.where(lane>=sub+8*q,u*rs,0.0)); put_l(q, l*rs)
def chol_kernel(g_ref, r_ref, a_ref, l_ref, d_ref, u_ref):
    a_ref[...]=g_ref[...]
    r_ref[...]=jnp.zeros_like(r_ref)
    def put_u(i,v): u_ref[8*i:8*i+8,:]=v
    def put_l(i,v): l_ref[8*i:8*i+8,:]=v
    def fac():
        factor_block(lambda i:d_ref[8*i:8*i+8,:],put_u,put_l)
    for k in range(NB):
        o=k*B
        d_ref[...]=a_ref[o:o+B,o:o+B]
        lax.fori_loop(0,1,lambda i,c:(fac(),c)[1],0)
        r_ref[o:o+B,o:o+B]=u_ref[...]
        if k<NB-1:
            p=dot(l_ref[...],a_ref[o:o+B,o+B:])
            r_ref[o:o+B,o+B:]=p
            for m in range(k+1,NB):
                x=m*B
                a_ref[x:x+B,x:]-=dotT(r_ref[o:o+B,x:x+B],r_ref[o:o+B,x:])
def upper_factor(g):
    return pl.pallas_call(chol_kernel,out_shape=jax.ShapeDtypeStruct((N,N),jnp.float32),
       in_specs=[pl.BlockSpec(memory_space=pltpu.VMEM)],out_specs=pl.BlockSpec(memory_space=pltpu.VMEM),
       scratch_shapes=[pltpu.VMEM((N,N),jnp.float32)]+[pltpu.VMEM((B,B),jnp.float32)]*3,
       compiler_params=pltpu.CompilerParams(vmem_limit_bytes=40<<20),name="upper_factor")(g)


def slots(ids):
    tokens = ids.shape[0]
    names = jnp.arange(experts, dtype=jnp.int32)
    named = jnp.any(ids[:, :, None] == names[None, None, :], axis=1)
    before = (jnp.arange(tokens)[:, None] > jnp.arange(tokens)[None, :]).astype(jnp.bfloat16)
    rank = jnp.dot(before, named.astype(jnp.bfloat16), preferred_element_type=jnp.float32)
    rank = jnp.where(named, rank.astype(jnp.int32), capacity).T
    rank = rank.reshape(16, 2, 2, 2, tokens).transpose(1, 3, 0, 2, 4).reshape(4, 32, tokens)
    slot = jnp.arange(capacity, dtype=jnp.int32)
    chosen = rank[:, :, None, :] == slot[None, None, :, None]
    return chosen.astype(jnp.bfloat16).reshape(4, 32 * capacity, tokens)


def exchange_kernel(tok, plc, w, rows, other, tok_all, plc_all, out, near_s, near_r, far_s, far_r, w_s, w_r, own):
    z, y, c = lax.axis_index("z"), lax.axis_index("y"), lax.axis_index("core")
    xh, xl = lax.axis_index("xh"), lax.axis_index("xl")
    me_x = xh * 2 + xl
    me_p = (z * 4 + y) * 2 + c

    def on_ring(r):
        p = (me_x + r) % 4
        return p, (z, y, p // 2, c, p % 2)

    def on_plane(k):
        p = (me_p + k) % 32
        return p, (p // 8, (p // 2) % 4, xh, p % 2, xl)

    barrier = pltpu.get_barrier_semaphore()
    for r in range(1, 4):
        pl.semaphore_signal(barrier, 1, device_id=on_ring(r)[1], device_id_type=MESH)

    def greet(k, carry):
        pl.semaphore_signal(barrier, 1, device_id=on_plane(k)[1], device_id_type=MESH)
        return carry

    lax.fori_loop(1, 32, greet, 0)
    pl.semaphore_wait(barrier, 34)

    near = []
    for r in range(1, 4):
        p, device = on_ring(r)
        near.append(
            pltpu.make_async_remote_copy(
                tok, tok_all.at[me_x], near_s.at[2 * r - 2], near_r.at[2 * r - 2], device_id=device, device_id_type=MESH
            )
        )
        near.append(
            pltpu.make_async_remote_copy(
                plc.at[p], plc_all.at[me_x], near_s.at[2 * r - 1], near_r.at[2 * r - 1], device_id=device, device_id_type=MESH
            )
        )
    for copy in near:
        copy.start()
    here = [
        pltpu.make_async_copy(tok, tok_all.at[me_x], own.at[0]),
        pltpu.make_async_copy(plc.at[me_x], plc_all.at[me_x], own.at[1]),
    ]
    for copy in here:
        copy.start()
    for copy in here:
        copy.wait()
    for copy in near:
        copy.wait()
    weights = [
        pltpu.make_async_remote_copy(
            w.at[1 - xl, :, pl.ds(i * part, part)],
            other.at[:, pl.ds(i * part, part)],
            w_s.at[i],
            w_r.at[i],
            device_id=(z, y, xh, c, 1 - xl),
            device_id_type=MESH,
        )
        for i in range(other.shape[1] // part)
    ]
    for copy in weights:
        copy.start()

    def select(i, carry):
        columns = pl.ds(pl.multiple_of(i * 512, 512), 512)
        picked = [
            jnp.dot(plc_all[b], tok_all[b, :, columns], preferred_element_type=jnp.float32).reshape(32, 8, 512)
            for b in range(4)
        ]
        out[:, columns] = jnp.stack(picked, axis=1).reshape(1024, 512).astype(jnp.bfloat16)
        return carry

    lax.fori_loop(0, 8, select, 0)

    def far(k):
        p, device = on_plane(k)
        return pltpu.make_async_remote_copy(
            out.at[pl.ds(pl.multiple_of(p * 32, 32), 32), :],
            rows.at[pl.ds(pl.multiple_of(me_p * 32, 32), 32), :],
            far_s.at[k],
            far_r.at[k],
            device_id=device,
            device_id_type=MESH,
        )

    def start(k, carry):
        far(k).start()
        return carry

    def finish(k, carry):
        far(k).wait()
        return carry

    lax.fori_loop(1, 32, start, 0)
    mine = pl.ds(pl.multiple_of(me_p * 32, 32), 32)
    kept = pltpu.make_async_copy(out.at[mine, :], rows.at[mine, :], own.at[0])
    kept.start()
    lax.fori_loop(1, 32, finish, 0)
    kept.wait()
    for copy in weights:
        copy.wait()


def exchange(tokens, placing, gate_up):
    depth = tokens.shape[1]
    anywhere = pl.BlockSpec(memory_space=pl.ANY)
    dma = pltpu.SemaphoreType.DMA
    return pl.pallas_call(
        exchange_kernel,
        out_shape=(
            jax.ShapeDtypeStruct((1024, depth), jnp.bfloat16),
            jax.ShapeDtypeStruct((depth, in_kernel), jnp.bfloat16),
        ),
        in_specs=[anywhere] * 3,
        out_specs=(anywhere, anywhere),
        scratch_shapes=[
            pltpu.VMEM((4, 64, depth), jnp.bfloat16),
            pltpu.VMEM((4, 256, 64), jnp.bfloat16),
            pltpu.VMEM((1024, depth), jnp.bfloat16),
            dma((6,)),
            dma((6,)),
            dma((32,)),
            dma((32,)),
            dma((6,)),
            dma((6,)),
            dma((2,)),
        ],
        compiler_params=pltpu.CompilerParams(collective_id=1, has_side_effects=True, vmem_limit_bytes=48 << 20),
        name="exchange",
    )(tokens, placing, gate_up)


def on_device(tokens, expert_ids, gate_up):
    xl = lax.axis_index("xl")
    width = gate_up.shape[2]
    placing = slots(expert_ids)
    rows, other = exchange(tokens, placing, gate_up)
    keep = lax.dynamic_index_in_dim(gate_up, xl, 0, keepdims=False)
    mine = jnp.dot(rows, keep, preferred_element_type=jnp.float32)
    theirs = jnp.dot(rows, other, preferred_element_type=jnp.float32)
    gate = jnp.where(xl == 0, mine, theirs)
    up = jnp.where(xl == 0, theirs, mine)
    hidden = (jax.nn.silu(gate) * up).astype(jnp.bfloat16)
    gram = lax.dot_general(hidden, hidden, (((0,), (0,)), ((), ())), preferred_element_type=jnp.float32)
    moment = gram * (1.0 / rows_mean) + damping * damping * jnp.eye(width, dtype=jnp.float32)
    factor = upper_factor(moment)
    half = width // 2
    away = lax.dynamic_slice_in_dim(factor, (1 - xl) * half, half, 0)
    here = lax.dynamic_slice_in_dim(factor, xl * half, half, 0)
    got = lax.ppermute(away, "xl", [(0, 1), (1, 0)])
    return jnp.stack([jnp.where(xl == 0, here, got), jnp.where(xl == 0, got, here)])


def solution(mesh):
    split = Mesh(mesh.devices.reshape(4, 4, 2, 2, 2), ("z", "y", "xh", "core", "xl"))
    every = ("z", "y", "xh", "core", "xl")
    holders = ("z", "y", "xh", "core")
    return jax.shard_map(
        on_device,
        mesh=split,
        in_specs=(P(every, None), P(every, None), P(holders, None, "xl")),
        out_specs=P(holders, "xl", None),
        check_vma=False,
    )
```

time: 378 us -> 274 us (0.72)
  the two profiles are of different devices: /device:TPU:1 before, /device:TPU:33 now
where the time goes in v2:
time: 274 us
  Pallas kernels  220 us (80%)
  waiting for transfers between devices  24.5 us (9%)
  matrix products  23.9 us (9%)
  local copies, waits for them, and re-layouts  3.13 us (1%)
    pallas_call x1, Pallas kernels, exchange(): pl.pallas_call(exchange_kernel, out_shape=(jax.ShapeDtypeStruct((1024, de...  190 us
    pallas_call x1, Pallas kernels, upper_factor(): pl.pallas_call(chol_kernel, out_shape=jax.ShapeDtypeStruct((N, N), jnp.fl...  30.6 us
    ppermute x1, waiting for transfers between devices, on_device(): got = lax.ppermute(away, 'xl', [(0, 1), (1, 0)])  24.5 us
    dot_general x1, matrix products, on_device(): mine = jnp.dot(rows, keep, preferred_element_type=jnp.float32)  11.5 us
    dot_general x1, matrix products, on_device(): theirs = jnp.dot(rows, other, preferred_element_type=jnp.float32)  10.9 us
  transfers between devices with their start and end apart: 1, of which 1 were waited for; matrix products, arithmetic and copies ran while one was open for 0% of the time, Pallas kernels for 0%

profile of v2, /device:TPU:33, one launch (start us, length us, event | category | flops | bytes accessed | tf_op | source)
XLA Modules:
  0.0 273.8 jit_solution(10527723581546396195)
XLA Ops:
  0.0 0.1 eq.52
  0.1 0.8 copy.8
  0.9 0.2 fusion.7
  1.0 0.1 fusion.5
  1.2 0.1 copy.9
  1.3 0.1 fusion.6.plc
  1.4 0.0 copy-start
  1.5 1.0 copy-done
  2.5 189.6 %exchange.1 = (bf16[1024,4096]{1,0:T(8,128)(2,1)}, bf16[4096,768]{1,0:T(8,128)(2,1)}) custom-call(bf16[64,4096]{1,0:T(8,128)(2,1)S(1)} %copy-done, bf16[4,256,64]{2,1,0:T(8,128)(2,1)S(1)} %fusion.6.plc, bf16[2,4096,768]{2,1,0:T(8,128)(2,1)} %w.1), custom_call_target="tpu_custom_call" | custom-call | tf_op jit(solution)/shard_map/exchange/pallas_call | solution.py:202
  192.1 10.9 %fusion.9 = f32[1024,768]{1,0:T(8,128)S(1)} fusion(bf16[1024,4096]{1,0:T(8,128)(2,1)} %get-tuple-element.7, bf16[4096,768]{1,0:T(8,128)(2,1)} %get-tuple-element.8), kind=kOutput, calls=%fused_computation.18 | convolution fusion | flops 6442450944 | bytes 17825792 | tf_op jit(solution)/shard_map/dot_general | solution.py:234
  203.0 11.5 %multiply_convert_fusion = bf16[1024,768]{1,0:T(8,128)(2,1)S(1)} fusion(f32[1024,768]{1,0:T(8,128)S(1)} %fusion.9, bf16[1024,4096]{1,0:T(8,128)(2,1)} %get-tuple-element.7, bf16[2,4096,768]{2,1,0:T(8,128)(2,1)} %w.1, s32[]{:T(128)S(6)} %select_n.42, pred[]{:T(512)S(6)} %eq.44), kind=kOutput, calls=%fused_computation.3 | convolution fusion | flops 6448742400 | bytes 19398660 | tf_op jit(solution)/shard_map/dot_general | solution.py:233
  214.5 1.4 select_add_fusion.g_ref
  215.9 30.6 %upper_factor.1 = f32[768,768]{1,0:T(8,128)S(1)} custom-call(f32[768,768]{1,0:T(8,128)S(1)} %select_add_fusion.g_ref), custom_call_target="tpu_custom_call" | custom-call | tf_op jit(solution)/shard_map/upper_factor/pallas_call | solution.py:75
  246.5 1.1 constant_dynamic-slice_fusion
  247.6 0.0 collective-permute-start
  247.6 24.5 %collective-permute-done = f32[384,768]{1,0:T(8,128)S(1)} collective-permute-done((f32[384,768]{1,0:T(8,128)}, f32[384,768]{1,0:T(8,128)S(1)}, u32[]{:S(2)}, u32[]{:S(2)}) %collective-permute-start) | collective-permute-done | bytes 1179680 | tf_op jit(solution)/shard_map/ppermute | solution.py:244
  272.1 0.2 select_bitcast_fusion.1
  272.3 1.6 pad_maximum_fusion
  (2 shorter events, 0.0 us)
Async XLA Ops:
  1.4 1.0 copy-start
  247.6 24.5 %collective-permute-start = (f32[384,768]{1,0:T(8,128)}, f32[384,768]{1,0:T(8,128)S(1)}, u32[]{:S(2)}, u32[]{:S(2)}) collective-permute-start(f32[384,768]{1,0:T(8,128)} %constant_dynamic-slice_fusion), channel_id=1, source_target_pairs={{0,1},{1,0},{2,3},{3,2},{4,5},{5,4},{6,7},{7,6},{8,9},{9,8},{10,11... | collective-permute-start | bytes 3538952 | tf_op jit(solution)/shard_map/ppermute | solution.py:244
